TPU v7x, 32 devices: a whole 2x2x4 slice. The times are simulated.
32 devices in a mesh: cuts: 4 (over y, x), det: 2 (over core), bank: 4 (over z).
Axes of the slice: x: 2, y: 2, z: 4, core: 2. Of those that a mesh axis runs over, the one named last changes fastest.
Arguments:
- strain: bfloat16 [4, 2, 6144], P('cuts', 'det'), may hold values from -6 to 6
- filters: bfloat16 [16, 256, 2048], P(('bank', 'cuts')), parts along dimension 0, may hold values from -0.125 to 0.125
- recon_weights: bfloat16 [16, 128, 256], P(('bank', 'cuts')), parts along dimension 0, may hold values from -0.1875 to 0.1875
- row_spans: int32 [512], P('bank'), parts along dimension 0, may hold values from 1 to 4
- slice_rates: int32 [4], replicated, may hold values from 1 to 8, as said below
- delays: int32 [64, 2], replicated, may hold values from 0 to 47
- antenna: float32 [64, 2], replicated, may hold values from 0.2 to 1
Outputs:
- peak_amplitude: float32 [512, 4096], P(('bank', 'cuts', 'det')), parts along dimension 0
There are 4 independent parts, one for each index of `bank`. A program takes and returns all parts, laid end to end along the dimension named above; an argument that names none is the same for every part. Nothing has to cross between parts.
Inputs may be any that keep to these rules, and one draw needn't show every extreme that they name: `slice_rates`: every entry is a power of two; entries never fall along the slices; the first is 1 and the last is 8.
All inputs are finite; a program needn't handle non-finite values.
Results may differ from a plain program's by a relative error of at most 0.0014.
Values sent between devices are 32-bit elements; how exact they have to be, the bound alone decides.
A program may use at most 64 MiB of HBM per device.

v0:
```python
import functools

import jax
import jax.numpy as jnp
from jax import lax
from jax.experimental import pallas as pl
from jax.experimental.pallas import tpu as pltpu
from jax.sharding import PartitionSpec as P

MESH = pl.DeviceIdType.MESH
LANES = 128
WIDE = 256
BATCH = 2
LEVELS = 4
CHUNK = 64


def exchange_kernel(
    cuts, dets, spans_ref, strain_ref, weights_ref, filters_hbm, bank_ref, series_ref,
    filters, bank_stage, series_stage, bank_send, bank_recv, cross_send, cross_recv, side_send, side_recv,
    local_sem,
):
    me = lax.axis_index("cuts")
    core = lax.axis_index("det")
    fetch = pltpu.make_async_copy(filters_hbm, filters, local_sem.at[0])
    fetch.start()
    barrier = pltpu.get_barrier_semaphore()
    for step in range(1, cuts):
        pl.semaphore_signal(
            barrier, inc=1, device_id={"cuts": lax.rem(me + step, cuts)}, device_id_type=MESH
        )
    for turn in range(1, dets):
        pl.semaphore_signal(
            barrier, inc=1, device_id={"det": lax.rem(core + turn, dets)}, device_id_type=MESH
        )

    series_stage[...] = strain_ref[...].astype(jnp.float32)
    rows = weights_ref.shape[0]
    share = rows // cuts // dets
    live = (me < spans_ref[...]).astype(jnp.float32)
    across = lax.broadcasted_iota(jnp.int32, (rows, rows), 1)
    down = lax.broadcasted_iota(jnp.int32, (rows, rows), 0)
    keep = jnp.sum(jnp.where(across == down, live, 0.0), axis=1, keepdims=True)
    kept = (weights_ref[...].astype(jnp.float32) * keep).astype(jnp.bfloat16)
    parts = []
    for cut in range(cuts):
        low = kept[(cut * dets) * share : (cut * dets + 1) * share]
        for det in range(1, dets):
            other = kept[(cut * dets + det) * share : (cut * dets + det + 1) * share]
            low = jnp.where(core == det, other, low)
        parts.append(low)
    stacked = jnp.concatenate(parts, axis=0)

    pl.semaphore_wait(barrier, cuts - 1 + dets - 1)
    mine = me * dets + core
    cross = []
    for step in range(1, cuts):
        cross.append(pltpu.make_async_remote_copy(
            src_ref=series_stage, dst_ref=series_ref.at[mine],
            send_sem=cross_send.at[step - 1], recv_sem=cross_recv.at[step - 1],
            device_id={"cuts": lax.rem(me + step, cuts)}, device_id_type=MESH,
        ))
    for copy in cross:
        copy.start()
    side = []
    for step in range(cuts):
        origin = lax.rem(me - step + cuts, cuts) * dets + core
        for turn in range(1, dets):
            number = step * (dets - 1) + turn - 1
            side.append(pltpu.make_async_remote_copy(
                src_ref=series_ref.at[origin] if step else series_stage, dst_ref=series_ref.at[origin],
                send_sem=side_send.at[number], recv_sem=side_recv.at[number],
                device_id={"det": lax.rem(core + turn, dets)}, device_id_type=MESH,
            ))
    for copy in side[: dets - 1]:
        copy.start()
    own = [
        pltpu.make_async_copy(series_stage, series_ref.at[mine], local_sem.at[1]),
        pltpu.make_async_copy(bank_stage.at[me], bank_ref.at[me], local_sem.at[2]),
    ]
    own[0].start()

    fetch.wait()
    taps = filters.shape[1]
    for first in range(0, taps, WIDE):
        block = jnp.dot(stacked, filters[:, first : first + WIDE], preferred_element_type=jnp.float32)
        for cut in range(cuts):
            bank_stage[cut, :, first : first + WIDE] = block[cut * share : (cut + 1) * share]
    banks = []
    for step in range(1, cuts):
        target = lax.rem(me + step, cuts)
        banks.append(pltpu.make_async_remote_copy(
            src_ref=bank_stage.at[target], dst_ref=bank_ref.at[me],
            send_sem=bank_send.at[step - 1], recv_sem=bank_recv.at[step - 1],
            device_id={"cuts": target}, device_id_type=MESH,
        ))
    for copy in banks:
        copy.start()
    own[1].start()
    for step in range(1, cuts):
        cross[step - 1].wait_recv()
        for turn in range(1, dets):
            side[step * (dets - 1) + turn - 1].start()
    for copy in own:
        copy.wait()
    for copy in cross:
        copy.wait_send()
    for copy in side:
        copy.wait()
    for copy in banks:
        copy.wait()


def exchange(spans, strain, filters, weights, cuts, dets):
    rows = weights.shape[0] // cuts // dets
    taps = filters.shape[1]
    length = strain.shape[-1]
    vmem = pl.BlockSpec(memory_space=pltpu.VMEM)
    hbm = pl.BlockSpec(memory_space=pltpu.HBM)
    dma = pltpu.SemaphoreType.DMA
    return pl.pallas_call(
        functools.partial(exchange_kernel, cuts, dets),
        out_shape=(
            jax.ShapeDtypeStruct((cuts, rows, taps), jnp.float32),
            jax.ShapeDtypeStruct((cuts * dets, 1, length), jnp.float32),
        ),
        in_specs=[vmem, vmem, vmem, hbm],
        out_specs=(hbm, hbm),
        scratch_shapes=[
            pltpu.VMEM(filters.shape, filters.dtype),
            pltpu.VMEM((cuts, rows, taps), jnp.float32),
            pltpu.VMEM((1, length), jnp.float32),
            dma((cuts - 1,)),
            dma((cuts - 1,)),
            dma((cuts - 1,)),
            dma((cuts - 1,)),
            dma((cuts * (dets - 1),)),
            dma((cuts * (dets - 1),)),
            dma((3,)),
        ],
        compiler_params=pltpu.CompilerParams(collective_id=0, has_side_effects=True),
    )(spans, strain, weights, filters)


def search_kernel(
    rates_ref, delays_ref, antenna_ref, bank_ref, series_ref, peak_ref,
    even, odd, total, combined, turned, best,
):
    slices, rows, taps = bank_ref.shape
    dets = series_ref.shape[0] // slices
    window = peak_ref.shape[1]
    tiles = window // LANES
    pieces = taps // WIDE
    chunks = series_ref.shape[2] // LANES
    combined[...] = jnp.zeros(combined.shape, jnp.float32)
    lane = lax.broadcasted_iota(jnp.int32, (rows, LANES), 1)
    ahead = lax.broadcasted_iota(jnp.int32, (LANES, LANES), 1) >= lax.broadcasted_iota(
        jnp.int32, (LANES, LANES), 0
    )

    def one_slice(number, carry):
        rate = rates_ref[number]
        level = (rate > 1).astype(jnp.int32) + (rate > 3).astype(jnp.int32) + (rate > 7).astype(jnp.int32)
        blocks = lax.shift_right_logical(jnp.int32(window // WIDE), level)
        batches = (blocks + pieces - 1 + 2 * BATCH - 1) // (2 * BATCH)
        taps_all = bank_ref[number].astype(jnp.bfloat16)
        stacked = jnp.concatenate(
            [taps_all[:, piece * WIDE : (piece + 1) * WIDE] for piece in range(pieces)], axis=0
        )
        for det in range(dets):
            for at in range(2 * (pieces - 1)):
                total[det, at] = jnp.zeros((rows, LANES), jnp.float32)

        def build(keep, first):
            for det in range(dets):
                before = None
                for near in range(2 * BATCH + 2):
                    at = pl.multiple_of(jnp.minimum(first + near, chunks - 1) * LANES, LANES)
                    piece = series_ref[number * dets + det, :, pl.ds(at, LANES)]
                    rolled = pltpu.roll(jnp.broadcast_to(piece, (LANES, LANES)), 0, 1, stride=1, stride_axis=0)
                    if near:
                        keep[det, near - 1] = jnp.where(ahead, rolled, before).astype(jnp.bfloat16)
                    before = rolled

        def multiply(keep, det, sums, start):
            for near in range(BATCH):
                low, middle, high = keep[det, 2 * near], keep[det, 2 * near + 1], keep[det, 2 * near + 2]
                square = jnp.concatenate(
                    [jnp.concatenate([middle, high], axis=1), jnp.concatenate([low, middle], axis=1)], axis=0
                )
                result = jnp.dot(stacked, square, preferred_element_type=jnp.float32)
                for piece in range(pieces):
                    term = result[piece * rows : (piece + 1) * rows]
                    old = sums[start + near + piece]
                    sums[start + near + piece] = term if old is None else old + term

        build(even, 0)

        def convolve(batch, c):
            base = 2 * BATCH * batch
            sums = [[None] * (2 * BATCH + pieces - 1) for det in range(dets)]
            build(odd, 2 * base + 2 * BATCH)
            for det in range(dets):
                multiply(even, det, sums[det], 0)
            build(even, 2 * base + 4 * BATCH)
            for det in range(dets):
                multiply(odd, det, sums[det], BATCH)
                for far, value in enumerate(sums[det]):
                    for half in range(2):
                        at = 2 * (base + far) + half
                        part = value[:, half * LANES : (half + 1) * LANES]
                        total[det, at] = part if far >= pieces - 1 else total[det, at] + part
            return c

        lax.fori_loop(0, batches, convolve, 0)

        skip = 2 * (pieces - 1)
        for known in range(LEVELS):
            @pl.when(level == known)
            def _(known=known):
                for tile in range(tiles):
                    index = lax.shift_right_logical(lane, known) + (tile % 2**known) * (LANES >> known)
                    for det in range(dets):
                        values = total[det, skip + (tile >> known)]
                        if known:
                            values = jnp.take_along_axis(values, index, axis=1)
                        combined[det, tile] += values
        return carry

    lax.fori_loop(0, slices, one_slice, 0)

    groups = LANES // rows
    apart = tiles // groups
    for det in range(dets):
        for offset in range(apart + 1):
            block = jnp.concatenate(
                [combined[det, group * apart + offset] for group in range(groups)], axis=0
            )
            turned[det, offset * LANES : (offset + 1) * LANES] = block.T

    for first in range(0, apart * LANES, CHUNK):
        def direction(number, highest):
            summed = None
            for det in range(dets):
                start = delays_ref[det, number] + first
                term = antenna_ref[det, number] * turned[det, pl.ds(start, CHUNK), :]
                summed = term if summed is None else summed + term
            return jnp.maximum(highest, jnp.abs(summed))

        best[first : first + CHUNK] = lax.fori_loop(
            0, delays_ref.shape[1], direction, jnp.zeros((CHUNK, LANES), jnp.float32), unroll=16
        )
    for offset in range(apart):
        back = best[offset * LANES : (offset + 1) * LANES].T
        for group in range(groups):
            at = (group * apart + offset) * LANES
            peak_ref[:, at : at + LANES] = back[group * rows : (group + 1) * rows]


def search(rates, delays, antenna, bank, series, window):
    slices, rows, taps = bank.shape
    dets = series.shape[0] // slices
    tiles = window // LANES
    pieces = taps // WIDE
    groups = LANES // rows
    apart = tiles // groups
    chunks = series.shape[2] // LANES
    smem = pl.BlockSpec(memory_space=pltpu.SMEM)
    vmem = pl.BlockSpec(memory_space=pltpu.VMEM)
    return pl.pallas_call(
        search_kernel,
        out_shape=jax.ShapeDtypeStruct((rows, window), jnp.float32),
        in_specs=[smem, smem, smem, vmem, vmem],
        out_specs=vmem,
        scratch_shapes=[
            pltpu.VMEM((dets, 2 * BATCH + 1, LANES, LANES), jnp.bfloat16),
            pltpu.VMEM((dets, 2 * BATCH + 1, LANES, LANES), jnp.bfloat16),
            pltpu.VMEM((dets, chunks + 4 * BATCH + 2 * pieces, rows, LANES), jnp.float32),
            pltpu.VMEM((dets, tiles + apart, rows, LANES), jnp.float32),
            pltpu.VMEM((dets, (apart + 1) * LANES, LANES), jnp.float32),
            pltpu.VMEM((apart * LANES, LANES), jnp.float32),
        ],
    )(rates, delays.T, antenna.T, bank, series)


def shards(strain, filters, recon_weights, row_spans, slice_rates, delays, antenna):
    cuts = lax.axis_size("cuts")
    dets = lax.axis_size("det")
    bank, series = exchange(
        row_spans.reshape(1, -1), strain.reshape(1, -1), filters[0], recon_weights[0], cuts, dets
    )
    window = strain.shape[-1] - filters.shape[-1]
    return search(slice_rates, delays, antenna, bank, series, window)


def solution(mesh):
    placed = (
        P("cuts", "det", None),
        P(("bank", "cuts"), None, None),
        P(("bank", "cuts"), None, None),
        P("bank"),
        P(),
        P(),
        P(),
    )
    return jax.shard_map(
        shards,
        mesh=mesh,
        in_specs=placed,
        out_specs=P(("bank", "cuts", "det"), None),
        check_vma=False,
    )
```

profile of v0, /device:TPU:0, one launch (start us, length us, event | category | flops | bytes accessed | tf_op | source)
XLA Modules:
  0.0 27.2 jit_solution(13820080385327760937)
XLA Ops:
  0.0 12.8 %shard_map.73 = (f32[4,16,2048]{2,1,0:T(8,128)}, f32[8,1,6144]{2,1,0:T(1,128)}) custom-call(s32[1,128]{1,0:T(1,128)} %bitcast.11, bf16[1,6144]{1,0:T(2,128)(2,1)} %bitcast.8, bf16[128,256]{1,0:T(8,128)(2,1)} %bitcast.7, bf16[256,2048]{1,0:T(8,128)(2,1)} %bitcast.6), custom_call_target="tpu_custom_call" | custom-call | tf_op jit(solution)/shard_map/pallas_call | solution.py:121
  12.8 14.4 %shard_map.74 = f32[16,4096]{1,0:T(8,128)} custom-call(s32[4]{0:T(128)} %rates_ref.1, s32[2,64]{1,0:T(2,128)} %bitcast.9, f32[2,64]{1,0:T(2,128)} %bitcast.10, f32[4,16,2048]{2,1,0:T(8,128)} %get-tuple-element.7.bank_ref, f32[8,1,6144]{2,1,0:T(1,128)} %get-tuple-element.8.series_ref), custom_call_target="tpu_custom_call" | custom-call | tf_op jit(solution)/shard_map/pallas_call | solution.py:270
where the time goes:
time: 27.5 us; the launch traced here: 27.2 us
  Pallas kernels  27.2 us (99%)
    pallas_call x1, Pallas kernels, search(): pl.pallas_call(search_kernel, out_shape=jax.ShapeDtypeStruct((rows, windo...  14.4 us
    pallas_call x1, Pallas kernels, exchange(): pl.pallas_call(functools.partial(exchange_kernel, cuts, dets), out_shape=...  12.8 us

commit v1 on v0

--- a/solution.py
+++ b/solution.py
@@ -144,7 +144,7 @@
 
 def search_kernel(
     rates_ref, delays_ref, antenna_ref, bank_ref, series_ref, peak_ref,
-    even, odd, total, combined, turned, best,
+    even, odd, last, total, combined, turned, best,
 ):
     slices, rows, taps = bank_ref.shape
     dets = series_ref.shape[0] // slices
@@ -171,16 +171,26 @@
             for at in range(2 * (pieces - 1)):
                 total[det, at] = jnp.zeros((rows, LANES), jnp.float32)
 
-        def build(keep, first):
+        def roll_of(det, at):
+            at = pl.multiple_of(jnp.minimum(at, chunks - 1) * LANES, LANES)
+            piece = series_ref[number * dets + det, :, pl.ds(at, LANES)]
+            return pltpu.roll(jnp.broadcast_to(piece, (LANES, LANES)), 0, 1, stride=1, stride_axis=0)
+
+        def build(keep, first, previous=None):
             for det in range(dets):
-                before = None
-                for near in range(2 * BATCH + 2):
-                    at = pl.multiple_of(jnp.minimum(first + near, chunks - 1) * LANES, LANES)
-                    piece = series_ref[number * dets + det, :, pl.ds(at, LANES)]
-                    rolled = pltpu.roll(jnp.broadcast_to(piece, (LANES, LANES)), 0, 1, stride=1, stride_axis=0)
-                    if near:
-                        keep[det, near - 1] = jnp.where(ahead, rolled, before).astype(jnp.bfloat16)
-                    before = rolled
+                if previous is None:
+                    before = roll_of(det, first)
+                    now = roll_of(det, first + 1)
+                    keep[det, 0] = jnp.where(ahead, now, before).astype(jnp.bfloat16)
+                    before = now
+                else:
+                    keep[det, 0] = previous[det, 2 * BATCH]
+                    before = last[det].astype(jnp.float32)
+                for near in range(1, 2 * BATCH + 1):
+                    now = roll_of(det, first + near + 1)
+                    keep[det, near] = jnp.where(ahead, now, before).astype(jnp.bfloat16)
+                    before = now
+                last[det] = before.astype(jnp.bfloat16)
 
         def multiply(keep, det, sums, start):
             for near in range(BATCH):
@@ -199,10 +209,10 @@
         def convolve(batch, c):
             base = 2 * BATCH * batch
             sums = [[None] * (2 * BATCH + pieces - 1) for det in range(dets)]
-            build(odd, 2 * base + 2 * BATCH)
+            build(odd, 2 * base + 2 * BATCH, even)
             for det in range(dets):
                 multiply(even, det, sums[det], 0)
-            build(even, 2 * base + 4 * BATCH)
+            build(even, 2 * base + 4 * BATCH, odd)
             for det in range(dets):
                 multiply(odd, det, sums[det], BATCH)
                 for far, value in enumerate(sums[det]):
@@ -275,6 +285,7 @@
         scratch_shapes=[
             pltpu.VMEM((dets, 2 * BATCH + 1, LANES, LANES), jnp.bfloat16),
             pltpu.VMEM((dets, 2 * BATCH + 1, LANES, LANES), jnp.bfloat16),
+            pltpu.VMEM((dets, LANES, LANES), jnp.bfloat16),
             pltpu.VMEM((dets, chunks + 4 * BATCH + 2 * pieces, rows, LANES), jnp.float32),
             pltpu.VMEM((dets, tiles + apart, rows, LANES), jnp.float32),
             pltpu.VMEM((dets, (apart + 1) * LANES, LANES), jnp.float32),

time: 27.5 us -> 26.8 us (0.975); the launches traced: 27.2 us -> 26.9 us
  Pallas kernels: 27.2 us -> 26.8 us
    pallas_call x1, Pallas kernels: 14.4 us -> 14 us  [search(): pl.pallas_call(search_kernel, out_shape=jax.ShapeDtypeStruct((rows, windo...]
where the time goes in v1:
time: 26.8 us; the launch traced here: 26.9 us
  Pallas kernels  26.8 us (100%)
    pallas_call x1, Pallas kernels, search(): pl.pallas_call(search_kernel, out_shape=jax.ShapeDtypeStruct((rows, windo...  14 us
    pallas_call x1, Pallas kernels, exchange(): pl.pallas_call(functools.partial(exchange_kernel, cuts, dets), out_shape=...  12.8 us

profile of v1, /device:TPU:0, one launch (start us, length us, event | category | flops | bytes accessed | tf_op | source)
XLA Modules:
  0.0 26.9 jit_solution(9963883406578097429)
XLA Ops:
  0.0 12.8 %shard_map.73 = (f32[4,16,2048]{2,1,0:T(8,128)}, f32[8,1,6144]{2,1,0:T(1,128)}) custom-call(s32[1,128]{1,0:T(1,128)} %bitcast.11, bf16[1,6144]{1,0:T(2,128)(2,1)} %bitcast.8, bf16[128,256]{1,0:T(8,128)(2,1)} %bitcast.7, bf16[256,2048]{1,0:T(8,128)(2,1)} %bitcast.6), custom_call_target="tpu_custom_call" | custom-call | tf_op jit(solution)/shard_map/pallas_call | solution.py:121
  12.8 14.0 %shard_map.74 = f32[16,4096]{1,0:T(8,128)} custom-call(s32[4]{0:T(128)} %rates_ref.1, s32[2,64]{1,0:T(2,128)} %bitcast.9, f32[2,64]{1,0:T(2,128)} %bitcast.10, f32[4,16,2048]{2,1,0:T(8,128)} %get-tuple-element.7.bank_ref, f32[8,1,6144]{2,1,0:T(1,128)} %get-tuple-element.8.series_ref), custom_call_target="tpu_custom_call" | custom-call | tf_op jit(solution)/shard_map/pallas_call | solution.py:280

commit v2 on v0

--- a/solution.py
+++ b/solution.py
@@ -144,7 +144,7 @@
 
 def search_kernel(
     rates_ref, delays_ref, antenna_ref, bank_ref, series_ref, peak_ref,
-    even, odd, total, combined, turned, best,
+    even, odd, last, total, combined, turned, best,
 ):
     slices, rows, taps = bank_ref.shape
     dets = series_ref.shape[0] // slices
@@ -158,29 +158,37 @@
         jnp.int32, (LANES, LANES), 0
     )
 
+    def build(keep, number, first, previous=None):
+        for det in range(dets):
+            if previous is not None:
+                keep[det, 0] = previous[det, 2 * BATCH]
+                before = last[det].astype(jnp.float32)
+            for near in range(1, 2 * BATCH + 1):
+                at = pl.multiple_of(jnp.clip(first + near + 1, 0, chunks - 1) * LANES, LANES)
+                piece = series_ref[number * dets + det, :, pl.ds(at, LANES)]
+                now = pltpu.roll(jnp.broadcast_to(piece, (LANES, LANES)), 0, 1, stride=1, stride_axis=0)
+                if previous is not None or near > 1:
+                    keep[det, near] = jnp.where(ahead, now, before).astype(jnp.bfloat16)
+                before = now
+            last[det] = before.astype(jnp.bfloat16)
+
+    for det in range(dets):
+        for near in range(2):
+            even[det, near] = jnp.zeros((LANES, LANES), jnp.bfloat16)
+    build(even, 0, -2)
+
     def one_slice(number, carry):
         rate = rates_ref[number]
         level = (rate > 1).astype(jnp.int32) + (rate > 3).astype(jnp.int32) + (rate > 7).astype(jnp.int32)
         blocks = lax.shift_right_logical(jnp.int32(window // WIDE), level)
-        batches = (blocks + pieces - 1 + 2 * BATCH - 1) // (2 * BATCH)
+        batches = (blocks + pieces + 2 * BATCH - 1) // (2 * BATCH)
         taps_all = bank_ref[number].astype(jnp.bfloat16)
         stacked = jnp.concatenate(
             [taps_all[:, piece * WIDE : (piece + 1) * WIDE] for piece in range(pieces)], axis=0
         )
         for det in range(dets):
-            for at in range(2 * (pieces - 1)):
+            for at in range(2 * pieces - 2):
                 total[det, at] = jnp.zeros((rows, LANES), jnp.float32)
-
-        def build(keep, first):
-            for det in range(dets):
-                before = None
-                for near in range(2 * BATCH + 2):
-                    at = pl.multiple_of(jnp.minimum(first + near, chunks - 1) * LANES, LANES)
-                    piece = series_ref[number * dets + det, :, pl.ds(at, LANES)]
-                    rolled = pltpu.roll(jnp.broadcast_to(piece, (LANES, LANES)), 0, 1, stride=1, stride_axis=0)
-                    if near:
-                        keep[det, near - 1] = jnp.where(ahead, rolled, before).astype(jnp.bfloat16)
-                    before = rolled
 
         def multiply(keep, det, sums, start):
             for near in range(BATCH):
@@ -194,15 +202,19 @@
                     old = sums[start + near + piece]
                     sums[start + near + piece] = term if old is None else old + term
 
-        build(even, 0)
-
         def convolve(batch, c):
             base = 2 * BATCH * batch
             sums = [[None] * (2 * BATCH + pieces - 1) for det in range(dets)]
-            build(odd, 2 * base + 2 * BATCH)
+            build(odd, number, 2 * base + 2 * BATCH - 2, even)
             for det in range(dets):
                 multiply(even, det, sums[det], 0)
-            build(even, 2 * base + 4 * BATCH)
+            final = batch == batches - 1
+            build(
+                even,
+                jnp.where(final, jnp.minimum(number + 1, slices - 1), number),
+                jnp.where(final, -2, 2 * base + 4 * BATCH - 2),
+                odd,
+            )
             for det in range(dets):
                 multiply(odd, det, sums[det], BATCH)
                 for far, value in enumerate(sums[det]):
@@ -214,7 +226,7 @@
 
         lax.fori_loop(0, batches, convolve, 0)
 
-        skip = 2 * (pieces - 1)
+        skip = 2 * pieces
         for known in range(LEVELS):
             @pl.when(level == known)
             def _(known=known):
@@ -275,6 +287,7 @@
         scratch_shapes=[
             pltpu.VMEM((dets, 2 * BATCH + 1, LANES, LANES), jnp.bfloat16),
             pltpu.VMEM((dets, 2 * BATCH + 1, LANES, LANES), jnp.bfloat16),
+            pltpu.VMEM((dets, LANES, LANES), jnp.bfloat16),
             pltpu.VMEM((dets, chunks + 4 * BATCH + 2 * pieces, rows, LANES), jnp.float32),
             pltpu.VMEM((dets, tiles + apart, rows, LANES), jnp.float32),
             pltpu.VMEM((dets, (apart + 1) * LANES, LANES), jnp.float32),

time: 27.5 us -> 25.5 us (0.927)
  Pallas kernels: 27.2 us -> 25.1 us
    pallas_call x1, Pallas kernels: 14.4 us -> 12.4 us  [search(): pl.pallas_call(search_kernel, out_shape=jax.ShapeDtypeStruct((rows, windo...]
where the time goes in v2:
time: 25.5 us; the launch traced here: 25.2 us
  Pallas kernels  25.1 us (98%)
    pallas_call x1, Pallas kernels, exchange(): pl.pallas_call(functools.partial(exchange_kernel, cuts, dets), out_shape=...  12.8 us
    pallas_call x1, Pallas kernels, search(): pl.pallas_call(search_kernel, out_shape=jax.ShapeDtypeStruct((rows, windo...  12.4 us

profile of v2, /device:TPU:0, one launch (start us, length us, event | category | flops | bytes accessed | tf_op | source)
XLA Modules:
  0.0 25.2 jit_solution(7267569984204827468)
XLA Ops:
  0.0 12.8 %shard_map.73 = (f32[4,16,2048]{2,1,0:T(8,128)}, f32[8,1,6144]{2,1,0:T(1,128)}) custom-call(s32[1,128]{1,0:T(1,128)} %bitcast.11, bf16[1,6144]{1,0:T(2,128)(2,1)} %bitcast.8, bf16[128,256]{1,0:T(8,128)(2,1)} %bitcast.7, bf16[256,2048]{1,0:T(8,128)(2,1)} %bitcast.6), custom_call_target="tpu_custom_call" | custom-call | tf_op jit(solution)/shard_map/pallas_call | solution.py:121
  12.8 12.4 %shard_map.74 = f32[16,4096]{1,0:T(8,128)} custom-call(s32[4]{0:T(128)} %rates_ref.1, s32[2,64]{1,0:T(2,128)} %bitcast.9, f32[2,64]{1,0:T(2,128)} %bitcast.10, f32[4,16,2048]{2,1,0:T(8,128)} %get-tuple-element.7.bank_ref, f32[8,1,6144]{2,1,0:T(1,128)} %get-tuple-element.8.series_ref), custom_call_target="tpu_custom_call" | custom-call | tf_op jit(solution)/shard_map/pallas_call | solution.py:282

commit v3 on v2

--- a/solution.py
+++ b/solution.py
@@ -16,14 +16,13 @@
 
 
 def exchange_kernel(
-    cuts, dets, spans_ref, strain_ref, weights_ref, filters_hbm, bank_ref, series_ref,
-    filters, bank_stage, series_stage, bank_send, bank_recv, cross_send, cross_recv, side_send, side_recv,
+    cuts, dets, spans_hbm, strain_hbm, weights_hbm, filters_hbm, bank_ref, series_ref,
+    spans_ref, strain_ref, weights_ref, filters, bank_stage, series_stage,
+    bank_send, bank_recv, cross_send, cross_recv, side_send, side_recv,
     local_sem,
 ):
     me = lax.axis_index("cuts")
     core = lax.axis_index("det")
-    fetch = pltpu.make_async_copy(filters_hbm, filters, local_sem.at[0])
-    fetch.start()
     barrier = pltpu.get_barrier_semaphore()
     for step in range(1, cuts):
         pl.semaphore_signal(
@@ -34,23 +33,16 @@
             barrier, inc=1, device_id={"det": lax.rem(core + turn, dets)}, device_id_type=MESH
         )
 
+    fetches = [
+        pltpu.make_async_copy(strain_hbm, strain_ref, local_sem.at[3]),
+        pltpu.make_async_copy(spans_hbm, spans_ref, local_sem.at[4]),
+        pltpu.make_async_copy(weights_hbm, weights_ref, local_sem.at[5]),
+        pltpu.make_async_copy(filters_hbm, filters, local_sem.at[0]),
+    ]
+    for copy in fetches:
+        copy.start()
+    fetches[0].wait()
     series_stage[...] = strain_ref[...].astype(jnp.float32)
-    rows = weights_ref.shape[0]
-    share = rows // cuts // dets
-    live = (me < spans_ref[...]).astype(jnp.float32)
-    across = lax.broadcasted_iota(jnp.int32, (rows, rows), 1)
-    down = lax.broadcasted_iota(jnp.int32, (rows, rows), 0)
-    keep = jnp.sum(jnp.where(across == down, live, 0.0), axis=1, keepdims=True)
-    kept = (weights_ref[...].astype(jnp.float32) * keep).astype(jnp.bfloat16)
-    parts = []
-    for cut in range(cuts):
-        low = kept[(cut * dets) * share : (cut * dets + 1) * share]
-        for det in range(1, dets):
-            other = kept[(cut * dets + det) * share : (cut * dets + det + 1) * share]
-            low = jnp.where(core == det, other, low)
-        parts.append(low)
-    stacked = jnp.concatenate(parts, axis=0)
-
     pl.semaphore_wait(barrier, cuts - 1 + dets - 1)
     mine = me * dets + core
     cross = []
@@ -80,7 +72,24 @@
     ]
     own[0].start()
 
-    fetch.wait()
+    fetches[1].wait()
+    fetches[2].wait()
+    rows = weights_ref.shape[0]
+    share = rows // cuts // dets
+    live = (me < spans_ref[...]).astype(jnp.float32)
+    across = lax.broadcasted_iota(jnp.int32, (rows, rows), 1)
+    down = lax.broadcasted_iota(jnp.int32, (rows, rows), 0)
+    keep = jnp.sum(jnp.where(across == down, live, 0.0), axis=1, keepdims=True)
+    kept = (weights_ref[...].astype(jnp.float32) * keep).astype(jnp.bfloat16)
+    parts = []
+    for cut in range(cuts):
+        low = kept[(cut * dets) * share : (cut * dets + 1) * share]
+        for det in range(1, dets):
+            other = kept[(cut * dets + det) * share : (cut * dets + det + 1) * share]
+            low = jnp.where(core == det, other, low)
+        parts.append(low)
+    stacked = jnp.concatenate(parts, axis=0)
+    fetches[3].wait()
     taps = filters.shape[1]
     for first in range(0, taps, WIDE):
         block = jnp.dot(stacked, filters[:, first : first + WIDE], preferred_element_type=jnp.float32)
@@ -115,7 +124,6 @@
     rows = weights.shape[0] // cuts // dets
     taps = filters.shape[1]
     length = strain.shape[-1]
-    vmem = pl.BlockSpec(memory_space=pltpu.VMEM)
     hbm = pl.BlockSpec(memory_space=pltpu.HBM)
     dma = pltpu.SemaphoreType.DMA
     return pl.pallas_call(
@@ -124,9 +132,12 @@
             jax.ShapeDtypeStruct((cuts, rows, taps), jnp.float32),
             jax.ShapeDtypeStruct((cuts * dets, 1, length), jnp.float32),
         ),
-        in_specs=[vmem, vmem, vmem, hbm],
+        in_specs=[hbm] * 4,
         out_specs=(hbm, hbm),
         scratch_shapes=[
+            pltpu.VMEM(spans.shape, spans.dtype),
+            pltpu.VMEM(strain.shape, strain.dtype),
+            pltpu.VMEM(weights.shape, weights.dtype),
             pltpu.VMEM(filters.shape, filters.dtype),
             pltpu.VMEM((cuts, rows, taps), jnp.float32),
             pltpu.VMEM((1, length), jnp.float32),
@@ -136,7 +147,7 @@
             dma((cuts - 1,)),
             dma((cuts * (dets - 1),)),
             dma((cuts * (dets - 1),)),
-            dma((3,)),
+            dma((6,)),
         ],
         compiler_params=pltpu.CompilerParams(collective_id=0, has_side_effects=True),
     )(spans, strain, weights, filters)

time: 25.5 us -> 24.8 us (0.973)
  Pallas kernels: 25.1 us -> 24.4 us
    pallas_call x1, Pallas kernels: 12.8 us -> 12 us  [exchange(): pl.pallas_call(functools.partial(exchange_kernel, cuts, dets), out_shape=...]
where the time goes in v3:
time: 24.8 us; the launch traced here: 24.4 us
  Pallas kernels  24.4 us (98%)
    pallas_call x1, Pallas kernels, search(): pl.pallas_call(search_kernel, out_shape=jax.ShapeDtypeStruct((rows, windo...  12.4 us
    pallas_call x1, Pallas kernels, exchange(): pl.pallas_call(functools.partial(exchange_kernel, cuts, dets), out_shape=...  12 us

profile of v3, /device:TPU:0, one launch (start us, length us, event | category | flops | bytes accessed | tf_op | source)
XLA Modules:
  0.0 24.4 jit_solution(512452515111194274)
XLA Ops:
  0.0 12.0 %shard_map.73 = (f32[4,16,2048]{2,1,0:T(8,128)}, f32[8,1,6144]{2,1,0:T(1,128)}) custom-call(s32[1,128]{1,0:T(1,128)} %bitcast.11, bf16[1,6144]{1,0:T(2,128)(2,1)} %bitcast.8, bf16[128,256]{1,0:T(8,128)(2,1)} %bitcast.7, bf16[256,2048]{1,0:T(8,128)(2,1)} %bitcast.6), custom_call_target="tpu_custom_call" | custom-call | tf_op jit(solution)/shard_map/pallas_call | solution.py:129
  12.0 12.4 %shard_map.74 = f32[16,4096]{1,0:T(8,128)} custom-call(s32[4]{0:T(128)} %rates_ref.1, s32[2,64]{1,0:T(2,128)} %bitcast.9, f32[2,64]{1,0:T(2,128)} %bitcast.10, f32[4,16,2048]{2,1,0:T(8,128)} %get-tuple-element.7.bank_ref, f32[8,1,6144]{2,1,0:T(1,128)} %get-tuple-element.8.series_ref), custom_call_target="tpu_custom_call" | custom-call | tf_op jit(solution)/shard_map/pallas_call | solution.py:293

commit v4 on v3

--- a/solution.py
+++ b/solution.py
@@ -154,9 +154,11 @@
 
 
 def search_kernel(
-    rates_ref, delays_ref, antenna_ref, bank_ref, series_ref, peak_ref,
-    even, odd, last, total, combined, turned, best,
+    rates_ref, delays_ref, antenna_ref, bank_hbm, series_ref, peak_ref,
+    bank_ref, bank_sem, even, odd, last, total, combined, turned, best,
 ):
+    fetch = pltpu.make_async_copy(bank_hbm, bank_ref, bank_sem)
+    fetch.start()
     slices, rows, taps = bank_ref.shape
     dets = series_ref.shape[0] // slices
     window = peak_ref.shape[1]
@@ -187,6 +189,7 @@
         for near in range(2):
             even[det, near] = jnp.zeros((LANES, LANES), jnp.bfloat16)
     build(even, 0, -2)
+    fetch.wait()
 
     def one_slice(number, carry):
         rate = rates_ref[number]
@@ -293,9 +296,11 @@
     return pl.pallas_call(
         search_kernel,
         out_shape=jax.ShapeDtypeStruct((rows, window), jnp.float32),
-        in_specs=[smem, smem, smem, vmem, vmem],
+        in_specs=[smem, smem, smem, pl.BlockSpec(memory_space=pltpu.HBM), vmem],
         out_specs=vmem,
         scratch_shapes=[
+            pltpu.VMEM(bank.shape, bank.dtype),
+            pltpu.SemaphoreType.DMA,
             pltpu.VMEM((dets, 2 * BATCH + 1, LANES, LANES), jnp.bfloat16),
             pltpu.VMEM((dets, 2 * BATCH + 1, LANES, LANES), jnp.bfloat16),
             pltpu.VMEM((dets, LANES, LANES), jnp.bfloat16),

time: 24.8 us -> 25.7 us (1.036)
  Pallas kernels: 24.4 us -> 25.5 us
    pallas_call x1, Pallas kernels: 12.4 us -> 13.5 us  [search(): pl.pallas_call(search_kernel, out_shape=jax.ShapeDtypeStruct((rows, windo...]
where the time goes in v4:
time: 25.7 us; the launch traced here: 25.5 us
  Pallas kernels  25.5 us (99%)
    pallas_call x1, Pallas kernels, search(): pl.pallas_call(search_kernel, out_shape=jax.ShapeDtypeStruct((rows, windo...  13.5 us
    pallas_call x1, Pallas kernels, exchange(): pl.pallas_call(functools.partial(exchange_kernel, cuts, dets), out_shape=...  12 us

profile of v4, /device:TPU:0, one launch (start us, length us, event | category | flops | bytes accessed | tf_op | source)
XLA Modules:
  0.0 25.5 jit_solution(7583397798850668382)
XLA Ops:
  0.0 12.0 %shard_map.73 = (f32[4,16,2048]{2,1,0:T(8,128)}, f32[8,1,6144]{2,1,0:T(1,128)}) custom-call(s32[1,128]{1,0:T(1,128)} %bitcast.11, bf16[1,6144]{1,0:T(2,128)(2,1)} %bitcast.8, bf16[128,256]{1,0:T(8,128)(2,1)} %bitcast.7, bf16[256,2048]{1,0:T(8,128)(2,1)} %bitcast.6), custom_call_target="tpu_custom_call" | custom-call | tf_op jit(solution)/shard_map/pallas_call | solution.py:129
  12.0 13.5 %shard_map.74 = f32[16,4096]{1,0:T(8,128)} custom-call(s32[4]{0:T(128)} %rates_ref.1, s32[2,64]{1,0:T(2,128)} %bitcast.9, f32[2,64]{1,0:T(2,128)} %bitcast.10, f32[4,16,2048]{2,1,0:T(8,128)} %get-tuple-element.7.bank_hbm, f32[8,1,6144]{2,1,0:T(1,128)} %get-tuple-element.8.series_ref), custom_call_target="tpu_custom_call" | custom-call | tf_op jit(solution)/shard_map/pallas_call | solution.py:296
